TPU v7x, 32 devices: a whole 2x2x4 slice. The times are simulated.
32 devices in a mesh: gx: 4 (over z), gy: 2 (over x), gz: 4 (over y, core).
Axes of the slice: x: 2, y: 2, z: 4, core: 2. Of those that a mesh axis runs over, the one named last changes fastest.
Arguments:
- volume: bfloat16 [64, 256, 512], P('gz', 'gy', 'gx'), may hold values from 0 to 1
- hat_center: int32 [256], replicated, may hold values from 0 to 255
- tf_table: bfloat16 [4, 256], replicated, may hold values from 0.049804688 to 1
Outputs:
- image: float32 [4, 256, 512], P(None, 'gy')
All inputs are finite; a program needn't handle non-finite values.
Results may differ from a plain program's by a relative error of at most 0.0003.
Values may be sent and summed in bfloat16 or wider, within the bound.
A program may use at most 64 MiB of HBM per device.

v0:
```python
import jax
import jax.numpy as jnp
from jax import lax
from jax.sharding import PartitionSpec as P

NBIN = 256
HW = 4


ambient = 0.3
grad_floor = 0.01
depth_scale = 1.5


def extended(cells, sides, width):
    for axis, dim in sides:
        count = lax.axis_size(axis)
        ends = count - 1
        head = lax.slice_in_dim(cells, 0, width, axis=dim)
        tail = lax.slice_in_dim(cells, cells.shape[dim] - width, cells.shape[dim], axis=dim)
        cells = jnp.concatenate(
            [
                lax.ppermute(tail, axis, [(i, (i + 1) % count) for i in range(ends)]),
                cells,
                lax.ppermute(head, axis, [((i + 1) % count, i) for i in range(ends)]),
            ],
            axis=dim,
        )
    return cells


def smooth(values, along):
    length = values.shape[along] - 2
    return (
        lax.slice_in_dim(values, 0, length, axis=along)
        + 2.0 * lax.slice_in_dim(values, 1, length + 1, axis=along)
        + lax.slice_in_dim(values, 2, length + 2, axis=along)
    )


def differ(values, along):
    length = values.shape[along] - 2
    return lax.slice_in_dim(values, 2, length + 2, axis=along) - lax.slice_in_dim(
        values, 0, length, axis=along
    )


def shading(padded):
    grad_x = smooth(smooth(differ(padded, 2), 1), 0) / 32.0
    grad_y = smooth(smooth(differ(padded, 1), 2), 0) / 32.0
    grad_z = smooth(smooth(differ(padded, 0), 2), 1) / 32.0
    facing = jnp.abs(grad_x + grad_y + grad_z) / jnp.sqrt(3.0)
    length = jnp.sqrt(grad_x * grad_x + grad_y * grad_y + grad_z * grad_z + grad_floor)
    return ambient + (1.0 - ambient) * facing / length


def colour(voxels, centers, tf_table):
    bin_level = voxels.astype(jnp.float32) * (NBIN - 1)
    hat_values = jnp.maximum(0.0, 1.0 - jnp.abs(bin_level[None, :] - centers[:, None]) / HW).astype(
        jnp.bfloat16
    )
    return jnp.dot(tf_table, hat_values, preferred_element_type=jnp.float32)


def fold_sources(stacked):
    through = jnp.cumprod(stacked[:, 3], axis=0)
    before = jnp.concatenate([jnp.ones_like(through[:1]), through[:-1]], axis=0)
    colour_sum = jnp.sum(before[:, None] * stacked[:, :3], axis=0)
    return jnp.concatenate([colour_sum, through[-1][None]], axis=0)


def finish(composed):
    return jnp.concatenate([composed[:3], 1.0 - composed[3:]], axis=0)


def display(band_piece):
    layers = lax.axis_size("gz")
    stacked = lax.all_gather(band_piece[None], ("gx", "gz"), axis=0, tiled=True)
    band_rows = band_piece.shape[1]
    across = band_piece.shape[2]
    stacked = stacked.reshape(stacked.shape[0] // layers, layers, 4, band_rows, across)
    stacked = jnp.transpose(stacked, (2, 1, 3, 0, 4))
    return stacked.reshape(4, layers * band_rows, stacked.shape[3] * across)


def shards(volume, hat_center, tf_table):
    planes, height, across = volume.shape
    layers = lax.axis_size("gz")
    total_depth = planes * layers
    padded = extended(volume, (("gx", 2), ("gy", 1), ("gz", 0)), 1)
    shading_term = shading(padded.astype(jnp.float32))
    centers = hat_center.astype(jnp.float32)
    transfer = lax.map(lambda slab_plane: colour(slab_plane.reshape(-1), centers, tf_table), volume)
    transfer = transfer.reshape(planes, 4, height, across)
    opacity = 1.0 - jnp.exp(-transfer[:, 3] * (depth_scale / total_depth))
    emitted = transfer[:, :3] * shading_term[:, None]
    through = jnp.cumprod(1.0 - opacity, axis=0)
    before = jnp.concatenate([jnp.ones_like(through[:1]), through[:-1]], axis=0)
    colour_sum = jnp.sum((before * opacity)[:, None] * emitted, axis=0)
    partial_value = jnp.concatenate([colour_sum, through[-1][None]], axis=0)
    band_rows = height // layers
    shaped = partial_value.reshape(1, 4, layers, band_rows, across)
    sources = lax.all_to_all(shaped, "gz", split_axis=2, concat_axis=0, tiled=True)
    sources = sources.reshape(layers, 4, band_rows, across)
    image_band = display(finish(fold_sources(sources)))
    return image_band


def solution(mesh):
    in_specs = (P("gz", "gy", "gx"), P(), P())
    out_specs = P(None, "gy", None)
    return jax.shard_map(shards, mesh=mesh, in_specs=in_specs, out_specs=out_specs, check_vma=False)
```

profile of v0, /device:TPU:0, one launch (start us, length us, event | category | flops | bytes accessed | tf_op | source)
XLA Modules:
  0.0 186.3 jit_solution(10785644348392411078)
XLA Ops:
  6.5 1.5 fusion.35
  8.0 5.0 %collective-permute-start = (bf16[16,128,1]{2,1,0:T(8,128)(2,1)S(1)}, bf16[16,128,1]{2,1,0:T(8,128)(2,1)S(1)}, u32[]{:S(2)}, u32[]{:S(2)}) collective-permute-start(bf16[16,128,1]{2,1,0:T(8,128)(2,1)S(1)} %get-tuple-element.47), channel_id=1, source_target_pairs={{0,8},{8,16},{16,24},{1,9},{9,17},{17,25},{2,10},{10,18},{18,26},{... | collective-permute-start | bytes 12296 | tf_op jit(solution)/shard_map/ppermute | solution.py:23
  13.0 1.3 collective-permute-start.1
  15.0 84.7 %while.10 = (s32[]{:T(128)}, f32[16,4,16384]{2,1,0:T(4,128)}, bf16[16,128,128]{2,1,0:T(8,128)(2,1)}, f32[256]{0:T(256)S(1)}, bf16[4,256]{1,0:T(4,128)(2,1)}, /*index=5*/s32[]{:T(128)}) while((s32[]{:T(128)}, f32[16,4,16384]{2,1,0:T(4,128)}, bf16[16,128,128]{2,1,0:T(8,128)(2,1)}, f32[256]{0:T(256)S(1)}, bf16[4,256]{1,0:T(4,128)(2,1)}, ...), condition=%wide.region_1.2_spmd, body=%wide.region_0.1_spmd.sunk | while | flops 58753024 | bytes 429641 | solution.py:93
  15.8 4.5 %fusion.41 = f32[16,4,16384]{2,1,0:T(4,128)} fusion(f32[16,4,16384]{2,1,0:T(4,128)} %get-tuple-element.89, s32[]{:T(128)} %get-tuple-element.88, bf16[4,256]{1,0:T(4,128)(2,1)} %get-tuple-element.98, f32[256]{0:T(256)S(1)} %get-tuple-element.97, f32[16384]{0:T(1024)S(1)} %multiply_bitcast_fusion.2), kind=kOutput, calls=%fused_computation.1.clone.1 | convolution fusion | flops 58720256 | bytes 331264 | tf_op jit(solution)/shard_map/while/body/eval_jaxpr/dot_general | solution.py:62
  21.1 4.5 %fusion.41 = f32[16,4,16384]{2,1,0:T(4,128)} fusion(f32[16,4,16384]{2,1,0:T(4,128)} %get-tuple-element.89, s32[]{:T(128)} %get-tuple-element.88, bf16[4,256]{1,0:T(4,128)(2,1)} %get-tuple-element.98, f32[256]{0:T(256)S(1)} %get-tuple-element.97, f32[16384]{0:T(1024)S(1)} %multiply_bitcast_fusion.2), kind=kOutput, calls=%fused_computation.1.clone.1 | convolution fusion | flops 58720256 | bytes 331264 | tf_op jit(solution)/shard_map/while/body/eval_jaxpr/dot_general | solution.py:62
  26.3 4.5 %fusion.41 = f32[16,4,16384]{2,1,0:T(4,128)} fusion(f32[16,4,16384]{2,1,0:T(4,128)} %get-tuple-element.89, s32[]{:T(128)} %get-tuple-element.88, bf16[4,256]{1,0:T(4,128)(2,1)} %get-tuple-element.98, f32[256]{0:T(256)S(1)} %get-tuple-element.97, f32[16384]{0:T(1024)S(1)} %multiply_bitcast_fusion.2), kind=kOutput, calls=%fused_computation.1.clone.1 | convolution fusion | flops 58720256 | bytes 331264 | tf_op jit(solution)/shard_map/while/body/eval_jaxpr/dot_general | solution.py:62
  31.6 4.5 %fusion.41 = f32[16,4,16384]{2,1,0:T(4,128)} fusion(f32[16,4,16384]{2,1,0:T(4,128)} %get-tuple-element.89, s32[]{:T(128)} %get-tuple-element.88, bf16[4,256]{1,0:T(4,128)(2,1)} %get-tuple-element.98, f32[256]{0:T(256)S(1)} %get-tuple-element.97, f32[16384]{0:T(1024)S(1)} %multiply_bitcast_fusion.2), kind=kOutput, calls=%fused_computation.1.clone.1 | convolution fusion | flops 58720256 | bytes 331264 | tf_op jit(solution)/shard_map/while/body/eval_jaxpr/dot_general | solution.py:62
  36.9 4.5 %fusion.41 = f32[16,4,16384]{2,1,0:T(4,128)} fusion(f32[16,4,16384]{2,1,0:T(4,128)} %get-tuple-element.89, s32[]{:T(128)} %get-tuple-element.88, bf16[4,256]{1,0:T(4,128)(2,1)} %get-tuple-element.98, f32[256]{0:T(256)S(1)} %get-tuple-element.97, f32[16384]{0:T(1024)S(1)} %multiply_bitcast_fusion.2), kind=kOutput, calls=%fused_computation.1.clone.1 | convolution fusion | flops 58720256 | bytes 331264 | tf_op jit(solution)/shard_map/while/body/eval_jaxpr/dot_general | solution.py:62
  42.2 4.5 %fusion.41 = f32[16,4,16384]{2,1,0:T(4,128)} fusion(f32[16,4,16384]{2,1,0:T(4,128)} %get-tuple-element.89, s32[]{:T(128)} %get-tuple-element.88, bf16[4,256]{1,0:T(4,128)(2,1)} %get-tuple-element.98, f32[256]{0:T(256)S(1)} %get-tuple-element.97, f32[16384]{0:T(1024)S(1)} %multiply_bitcast_fusion.2), kind=kOutput, calls=%fused_computation.1.clone.1 | convolution fusion | flops 58720256 | bytes 331264 | tf_op jit(solution)/shard_map/while/body/eval_jaxpr/dot_general | solution.py:62
  47.5 4.5 %fusion.41 = f32[16,4,16384]{2,1,0:T(4,128)} fusion(f32[16,4,16384]{2,1,0:T(4,128)} %get-tuple-element.89, s32[]{:T(128)} %get-tuple-element.88, bf16[4,256]{1,0:T(4,128)(2,1)} %get-tuple-element.98, f32[256]{0:T(256)S(1)} %get-tuple-element.97, f32[16384]{0:T(1024)S(1)} %multiply_bitcast_fusion.2), kind=kOutput, calls=%fused_computation.1.clone.1 | convolution fusion | flops 58720256 | bytes 331264 | tf_op jit(solution)/shard_map/while/body/eval_jaxpr/dot_general | solution.py:62
  52.8 4.5 %fusion.41 = f32[16,4,16384]{2,1,0:T(4,128)} fusion(f32[16,4,16384]{2,1,0:T(4,128)} %get-tuple-element.89, s32[]{:T(128)} %get-tuple-element.88, bf16[4,256]{1,0:T(4,128)(2,1)} %get-tuple-element.98, f32[256]{0:T(256)S(1)} %get-tuple-element.97, f32[16384]{0:T(1024)S(1)} %multiply_bitcast_fusion.2), kind=kOutput, calls=%fused_computation.1.clone.1 | convolution fusion | flops 58720256 | bytes 331264 | tf_op jit(solution)/shard_map/while/body/eval_jaxpr/dot_general | solution.py:62
  58.1 4.5 %fusion.41 = f32[16,4,16384]{2,1,0:T(4,128)} fusion(f32[16,4,16384]{2,1,0:T(4,128)} %get-tuple-element.89, s32[]{:T(128)} %get-tuple-element.88, bf16[4,256]{1,0:T(4,128)(2,1)} %get-tuple-element.98, f32[256]{0:T(256)S(1)} %get-tuple-element.97, f32[16384]{0:T(1024)S(1)} %multiply_bitcast_fusion.2), kind=kOutput, calls=%fused_computation.1.clone.1 | convolution fusion | flops 58720256 | bytes 331264 | tf_op jit(solution)/shard_map/while/body/eval_jaxpr/dot_general | solution.py:62
  63.4 4.5 %fusion.41 = f32[16,4,16384]{2,1,0:T(4,128)} fusion(f32[16,4,16384]{2,1,0:T(4,128)} %get-tuple-element.89, s32[]{:T(128)} %get-tuple-element.88, bf16[4,256]{1,0:T(4,128)(2,1)} %get-tuple-element.98, f32[256]{0:T(256)S(1)} %get-tuple-element.97, f32[16384]{0:T(1024)S(1)} %multiply_bitcast_fusion.2), kind=kOutput, calls=%fused_computation.1.clone.1 | convolution fusion | flops 58720256 | bytes 331264 | tf_op jit(solution)/shard_map/while/body/eval_jaxpr/dot_general | solution.py:62
  68.7 4.5 %fusion.41 = f32[16,4,16384]{2,1,0:T(4,128)} fusion(f32[16,4,16384]{2,1,0:T(4,128)} %get-tuple-element.89, s32[]{:T(128)} %get-tuple-element.88, bf16[4,256]{1,0:T(4,128)(2,1)} %get-tuple-element.98, f32[256]{0:T(256)S(1)} %get-tuple-element.97, f32[16384]{0:T(1024)S(1)} %multiply_bitcast_fusion.2), kind=kOutput, calls=%fused_computation.1.clone.1 | convolution fusion | flops 58720256 | bytes 331264 | tf_op jit(solution)/shard_map/while/body/eval_jaxpr/dot_general | solution.py:62
  74.0 4.5 %fusion.41 = f32[16,4,16384]{2,1,0:T(4,128)} fusion(f32[16,4,16384]{2,1,0:T(4,128)} %get-tuple-element.89, s32[]{:T(128)} %get-tuple-element.88, bf16[4,256]{1,0:T(4,128)(2,1)} %get-tuple-element.98, f32[256]{0:T(256)S(1)} %get-tuple-element.97, f32[16384]{0:T(1024)S(1)} %multiply_bitcast_fusion.2), kind=kOutput, calls=%fused_computation.1.clone.1 | convolution fusion | flops 58720256 | bytes 331264 | tf_op jit(solution)/shard_map/while/body/eval_jaxpr/dot_general | solution.py:62
  79.3 4.5 %fusion.41 = f32[16,4,16384]{2,1,0:T(4,128)} fusion(f32[16,4,16384]{2,1,0:T(4,128)} %get-tuple-element.89, s32[]{:T(128)} %get-tuple-element.88, bf16[4,256]{1,0:T(4,128)(2,1)} %get-tuple-element.98, f32[256]{0:T(256)S(1)} %get-tuple-element.97, f32[16384]{0:T(1024)S(1)} %multiply_bitcast_fusion.2), kind=kOutput, calls=%fused_computation.1.clone.1 | convolution fusion | flops 58720256 | bytes 331264 | tf_op jit(solution)/shard_map/while/body/eval_jaxpr/dot_general | solution.py:62
  84.6 4.5 %fusion.41 = f32[16,4,16384]{2,1,0:T(4,128)} fusion(f32[16,4,16384]{2,1,0:T(4,128)} %get-tuple-element.89, s32[]{:T(128)} %get-tuple-element.88, bf16[4,256]{1,0:T(4,128)(2,1)} %get-tuple-element.98, f32[256]{0:T(256)S(1)} %get-tuple-element.97, f32[16384]{0:T(1024)S(1)} %multiply_bitcast_fusion.2), kind=kOutput, calls=%fused_computation.1.clone.1 | convolution fusion | flops 58720256 | bytes 331264 | tf_op jit(solution)/shard_map/while/body/eval_jaxpr/dot_general | solution.py:62
  89.9 4.5 %fusion.41 = f32[16,4,16384]{2,1,0:T(4,128)} fusion(f32[16,4,16384]{2,1,0:T(4,128)} %get-tuple-element.89, s32[]{:T(128)} %get-tuple-element.88, bf16[4,256]{1,0:T(4,128)(2,1)} %get-tuple-element.98, f32[256]{0:T(256)S(1)} %get-tuple-element.97, f32[16384]{0:T(1024)S(1)} %multiply_bitcast_fusion.2), kind=kOutput, calls=%fused_computation.1.clone.1 | convolution fusion | flops 58720256 | bytes 331264 | tf_op jit(solution)/shard_map/while/body/eval_jaxpr/dot_general | solution.py:62
  95.2 4.5 %fusion.41 = f32[16,4,16384]{2,1,0:T(4,128)} fusion(f32[16,4,16384]{2,1,0:T(4,128)} %get-tuple-element.89, s32[]{:T(128)} %get-tuple-element.88, bf16[4,256]{1,0:T(4,128)(2,1)} %get-tuple-element.98, f32[256]{0:T(256)S(1)} %get-tuple-element.97, f32[16384]{0:T(1024)S(1)} %multiply_bitcast_fusion.2), kind=kOutput, calls=%fused_computation.1.clone.1 | convolution fusion | flops 58720256 | bytes 331264 | tf_op jit(solution)/shard_map/while/body/eval_jaxpr/dot_general | solution.py:62
  99.7 6.1 %reshape.44 = f32[16,4,128,128]{3,2,1,0:T(8,128)} reshape(f32[16,4,16384]{2,1,0:T(4,128)} %get-tuple-element.32) | data formatting | bytes 8388608 | tf_op jit(solution)/shard_map/reshape | solution.py:94
  105.9 3.4 %collective-permute-start.2 = (bf16[16,1,130]{2,1,0:T(2,128)(2,1)S(1)}, bf16[16,1,130]{2,1,0:T(2,128)(2,1)S(1)}, u32[]{:S(2)}, u32[]{:S(2)}) collective-permute-start(bf16[16,1,130]{2,1,0:T(2,128)(2,1)S(1)} %get-tuple-element.45), channel_id=1, source_target_pairs={{0,4},{1,5},{2,6},{3,7},{8,12},{9,13},{10,14},{11,15},{16,20},{17,... | collective-permute-start | bytes 12488 | tf_op jit(solution)/shard_map/ppermute | solution.py:23
  109.4 1.6 collective-permute-start.3
  110.9 1.4 fusion.25
  112.5 2.8 %collective-permute-done.3 = bf16[16,1,130]{2,1,0:T(2,128)(2,1)S(1)} collective-permute-done((bf16[16,1,130]{2,1,0:T(2,128)(2,1)S(1)}, bf16[16,1,130]{2,1,0:T(2,128)(2,1)S(1)}, u32[]{:S(2)}, u32[]{:S(2)}) %collective-permute-start.3) | collective-permute-done | bytes 4192 | tf_op jit(solution)/shard_map/ppermute | solution.py:25
  115.4 1.3 collective-permute-start.4
  116.7 1.3 collective-permute-start.5
  118.2 3.4 %collective-permute-done.5 = bf16[1,130,130]{2,1,0:T(8,128)(2,1)S(1)} collective-permute-done((bf16[1,130,130]{2,1,0:T(8,128)(2,1)S(1)}, bf16[1,130,130]{2,1,0:T(8,128)(2,1)S(1)}, u32[]{:S(2)}, u32[]{:S(2)}) %collective-permute-start.5) | collective-permute-done | bytes 33832 | tf_op jit(solution)/shard_map/ppermute | solution.py:25
  126.9 10.0 %all_to_all.15 = f32[1,4,4,32,128]{4,3,1,0,2:T(8,128)S(1)} all-to-all(f32[1,4,4,32,128]{4,3,1,0,2:T(8,128)S(1)} %copy.11), channel_id=1, replica_groups=mesh['gx'=4,'gy'=2,'gz'=4] {'gz'}, dimensions={2} | all-to-all | bytes 524288 | tf_op jit(solution)/shard_map/all_to_all | solution.py:103
  137.7 38.5 %all-gather.3.cloned.1.call-done = f32[64,32,128]{2,1,0:T(8,128)} async-done(((f32[4,32,128]{2,1,0:T(8,128)}), f32[64,32,128]{2,1,0:T(8,128)}) %all-gather.3.cloned.1.call-update) | async-done | bytes 1048592 | tf_op jit(solution)/shard_map/all_gather | solution.py:78
  176.2 1.9 %copy.12 = f32[4,4,32,4,128]{4,3,2,1,0:T(4,128)S(1)} copy(f32[4,4,32,4,128]{4,2,0,1,3:T(8,128)} %bitcast.53) | data formatting | bytes 2097152 | tf_op jit(solution)/shard_map/transpose | solution.py:82
  178.1 1.4 reshape.41
  (52 shorter events, 19.4 us)
Async XLA Ops:
  6.5 169.6 %all-gather.3.cloned.1.call-start = ((), (), s32[]{:S(2)}) async-start(), calls=%async_computation.1 | async-start | bytes 1114112 | tf_op jit(solution)/shard_map/all_gather | solution.py:78
  8.0 97.8 %collective-permute-start = (bf16[16,128,1]{2,1,0:T(8,128)(2,1)S(1)}, bf16[16,128,1]{2,1,0:T(8,128)(2,1)S(1)}, u32[]{:S(2)}, u32[]{:S(2)}) collective-permute-start(bf16[16,128,1]{2,1,0:T(8,128)(2,1)S(1)} %get-tuple-element.47), channel_id=1, source_target_pairs={{0,8},{8,16},{16,24},{1,9},{9,17},{17,25},{2,10},{10,18},{18,26},{... | collective-permute-start | bytes 12296 | tf_op jit(solution)/shard_map/ppermute | solution.py:23
  13.0 92.8 %collective-permute-start.1 = (bf16[16,128,1]{2,1,0:T(8,128)(2,1)S(1)}, bf16[16,128,1]{2,1,0:T(8,128)(2,1)S(1)}, u32[]{:S(2)}, u32[]{:S(2)}) collective-permute-start(bf16[16,128,1]{2,1,0:T(8,128)(2,1)S(1)} %get-tuple-element.48), channel_id=1, source_target_pairs={{8,0},{16,8},{24,16},{9,1},{17,9},{25,17},{10,2},{18,10},{26,18},{... | collective-permute-start | bytes 12296 | tf_op jit(solution)/shard_map/ppermute | solution.py:25
  99.7 6.1 %copy-start.1 = (bf16[16,128,128]{2,1,0:T(8,128)(2,1)S(1)}, bf16[16,128,128]{2,1,0:T(8,128)(2,1)}, u32[]{:S(2)}) copy-start(bf16[16,128,128]{2,1,0:T(8,128)(2,1)} %get-tuple-element.101) | copy-start | bytes 1572868
  105.9 6.5 %collective-permute-start.2 = (bf16[16,1,130]{2,1,0:T(2,128)(2,1)S(1)}, bf16[16,1,130]{2,1,0:T(2,128)(2,1)S(1)}, u32[]{:S(2)}, u32[]{:S(2)}) collective-permute-start(bf16[16,1,130]{2,1,0:T(2,128)(2,1)S(1)} %get-tuple-element.45), channel_id=1, source_target_pairs={{0,4},{1,5},{2,6},{3,7},{8,12},{9,13},{10,14},{11,15},{16,20},{17,... | collective-permute-start | bytes 12488 | tf_op jit(solution)/shard_map/ppermute | solution.py:23
  109.4 8.6 %copy-start = (f32[16,4,128,128]{3,2,1,0:T(8,128)S(1)}, f32[16,4,128,128]{3,2,1,0:T(8,128)}, u32[]{:S(2)}) copy-start(f32[16,4,128,128]{3,2,1,0:T(8,128)} %reshape.44) | copy-start | bytes 12582916
  109.4 5.9 %collective-permute-start.3 = (bf16[16,1,130]{2,1,0:T(2,128)(2,1)S(1)}, bf16[16,1,130]{2,1,0:T(2,128)(2,1)S(1)}, u32[]{:S(2)}, u32[]{:S(2)}) collective-permute-start(bf16[16,1,130]{2,1,0:T(2,128)(2,1)S(1)} %get-tuple-element.46), channel_id=1, source_target_pairs={{4,0},{5,1},{6,2},{7,3},{12,8},{13,9},{14,10},{15,11},{20,16},{21,... | collective-permute-start | bytes 12488 | tf_op jit(solution)/shard_map/ppermute | solution.py:25
  112.4 5.8 %copy-start.2 = (f32[16,128,128]{2,1,0:T(8,128)}, f32[16,128,128]{2,1,0:T(8,128)S(1)}, u32[]{:S(2)}) copy-start(f32[16,128,128]{2,1,0:T(8,128)S(1)} %fusion.25) | copy-start | bytes 3145732
  115.4 2.8 %collective-permute-start.4 = (bf16[1,130,130]{2,1,0:T(8,128)(2,1)S(1)}, bf16[1,130,130]{2,1,0:T(8,128)(2,1)S(1)}, u32[]{:S(2)}, u32[]{:S(2)}) collective-permute-start(bf16[1,130,130]{2,1,0:T(8,128)(2,1)S(1)} %get-tuple-element.43), channel_id=1, source_target_pairs={{0,1},{1,2},{2,3},{4,5},{5,6},{6,7},{8,9},{9,10},{10,11},{12,13},{... | collective-permute-start | bytes 101408 | tf_op jit(solution)/shard_map/ppermute | solution.py:23
  116.7 4.9 %collective-permute-start.5 = (bf16[1,130,130]{2,1,0:T(8,128)(2,1)S(1)}, bf16[1,130,130]{2,1,0:T(8,128)(2,1)S(1)}, u32[]{:S(2)}, u32[]{:S(2)}) collective-permute-start(bf16[1,130,130]{2,1,0:T(8,128)(2,1)S(1)} %get-tuple-element.44), channel_id=1, source_target_pairs={{1,0},{2,1},{3,2},{5,4},{6,5},{7,6},{9,8},{10,9},{11,10},{13,12},{... | collective-permute-start | bytes 101408 | tf_op jit(solution)/shard_map/ppermute | solution.py:25
  126.0 0.8 slice-start
Sparse Core Ops, SparseCore 0:
  137.8 38.2 all-gather.2
where the time goes:
time: 188 us; the launch traced here: 186 us
  matrix products  72.4 us (39%)
  waiting for transfers between devices  44.7 us (24%)
  other arithmetic  20.4 us (11%)
  starting transfers between devices  13.8 us (7%)
  between operations  13.6 us (7%)
  local copies, waits for them, and re-layouts  11.3 us (6%)
  blocking collectives  10 us (5%)
    dot_general x16, matrix products, colour(): return jnp.dot(tf_table, hat_values, preferred_element_type=jnp.float32)  72.4 us
    all_gather x1, waiting for transfers between devices, display(): stacked = lax.all_gather(band_piece[None], ('gx', 'gz'), axis=0, tiled=True)  38.5 us
    mul x16, other arithmetic, colour(): bin_level = voxels.astype(jnp.float32) * (NBIN - 1)  12.2 us
    all_to_all x1, blocking collectives, shards(): lax.all_to_all(shaped, 'gz', split_axis=2, concat_axis=0, tiled=True)  10 us
    ppermute x3, starting transfers between devices, extended(): lax.ppermute(tail, axis, [(i, (i + 1) % count) for i in range(ends)])  9.68 us
    ppermute x3, waiting for transfers between devices, extended(): lax.ppermute(head, axis, [((i + 1) % count, i) for i in range(ends)])  6.18 us
    reshape x1, local copies, waits for them, and re-layouts, shards(): transfer = transfer.reshape(planes, 4, height, across)  6.14 us
    ppermute x3, starting transfers between devices, extended(): lax.ppermute(head, axis, [((i + 1) % count, i) for i in range(ends)])  4.14 us
  transfers between devices with their start and end apart: 7, of which 3 were waited for; matrix products, arithmetic and copies ran while one was open for 50% of the time, Pallas kernels for 0%

commit v1 on v0

v1 whole, which is shorter than its diff:
```python
import functools

import jax
import jax.numpy as jnp
from jax import lax
from jax.experimental import pallas as pl
from jax.experimental.pallas import tpu as pltpu
from jax.sharding import PartitionSpec as P

NBIN = 256
HW = 4

ambient = 0.3
grad_floor = 0.01
depth_scale = 1.5

LANES = 128
BINADES = 8
GROUPS = BINADES + 5
MESH = pl.DeviceIdType.MESH
F32 = jnp.float32
BF16 = jnp.bfloat16


def build_tables(center_ref, table_ref, tab):
    centers = center_ref[...].astype(F32)
    wide = table_ref[...].astype(F32)
    copies = jnp.concatenate(
        [jnp.broadcast_to(wide[c : c + 1], (8, NBIN)) for c in range(4)], axis=0
    ).astype(BF16)
    centers = jnp.broadcast_to(centers, (LANES, NBIN))
    step = lax.broadcasted_iota(jnp.int32, (LANES, NBIN), 0).astype(F32) + float(LANES)

    def hats(level):
        return jnp.maximum(0.0, 1.0 - jnp.abs(level - centers) / HW)

    for group in range(GROUPS):
        if group < BINADES:
            weights = hats(step * (2.0 ** -(group + 8)) * (NBIN - 1))
        elif group == BINADES:
            weights = jnp.maximum(0.0, 1.0 - centers / HW)
        elif group == BINADES + 1:
            weights = jnp.where(centers == 0.0, -1.0, jnp.where(centers <= 2.0, 1.0, 0.0))
        elif group == BINADES + 2:
            weights = jnp.where(centers == 3.0, 1.0, 0.0)
        elif group == BINADES + 3:
            weights = jnp.where(centers == 4.0, 1.0, 0.0)
        else:
            weights = hats(jnp.full((LANES, NBIN), float(NBIN - 1), F32))
        tab[:, group * LANES : (group + 1) * LANES] = lax.dot_general(
            copies, weights.astype(BF16), (((1,), (1,)), ((), ())), preferred_element_type=F32
        )


def lookup(values, tab):
    masks = [values >= 2.0 ** -(k + 1) for k in range(BINADES)]
    scale = jnp.full(values.shape, 2.0 ** (BINADES + 7), F32)
    for k in range(BINADES - 2, -1, -1):
        scale = jnp.where(masks[k], 2.0 ** (k + 8), scale)
    index = (values * scale).astype(jnp.int32) & (LANES - 1)
    quarter = values * ((NBIN - 1) / 4.0)
    coarse = (quarter + 1.5 * 2.0**15) - 1.5 * 2.0**15
    fine = (quarter + 1.5 * 2.0**14) - 1.5 * 2.0**14
    finest = quarter.astype(BF16).astype(F32)
    top = values >= 1.0
    out = []
    for c in range(4):

        def entry(group):
            return tab[8 * c : 8 * c + 8, group * LANES : (group + 1) * LANES]

        total = entry(BINADES) + coarse * entry(BINADES + 1)
        total = total + fine * entry(BINADES + 2) + finest * entry(BINADES + 3)
        for k in range(BINADES - 1, -1, -1):
            total = jnp.where(masks[k], jnp.take_along_axis(entry(k), index, axis=1), total)
        out.append(jnp.where(top, entry(BINADES + 4), total))
    return out


def body(sizes, vol, center_ref, table_ref, out, tab, xsd, look, zhalo, face, faces, rows_out, rows_in, part, recv1, recv2, bit_a,
         zs, zr, fs, fr, rs, rr, es, er, us, ur, ds, dr, ys, yr, cs, cr, qs, qr):
    nx, ny, nz = sizes
    planes, height, across = vol.shape
    ix, iy, iz = lax.axis_index("gx"), lax.axis_index("gy"), lax.axis_index("gz")
    depth = planes * nz

    def at(x, y, z):
        return (x, y, z)

    relations = []
    for s in (-1, 1):
        relations.append((((ix + s >= 0) & (ix + s < nx)), (ix + s, iy, iz)))
        relations.append((((iz + s >= 0) & (iz + s < nz)), (ix, iy, iz + s)))
    for s in (-1, 1):
        for t in (-1, 0, 1):
            relations.append(
                ((iy + s >= 0) & (iy + s < ny) & (ix + t >= 0) & (ix + t < nx), (ix + t, iy + s, iz))
            )
    bit0, bit1 = iz % 2, iz // 2
    near = iz + 1 - 2 * bit0
    far = iz + 2 - 4 * bit1
    faces[...] = jnp.zeros_like(faces)
    rows_in[...] = jnp.zeros_like(rows_in)
    barrier = pltpu.get_barrier_semaphore()
    count = 2
    for there, where in relations:
        count = count + there.astype(jnp.int32)

        @pl.when(there)
        def _(where=where):
            pl.semaphore_signal(barrier, inc=1, device_id=where, device_id_type=MESH)

    for where in ((ix, iy, near), (ix, iy, far)):
        pl.semaphore_signal(barrier, inc=1, device_id=where, device_id_type=MESH)
    pl.semaphore_wait(barrier, count)

    def remote(src, dst, ssem, rsem, where):
        return pltpu.make_async_remote_copy(
            src_ref=src, dst_ref=dst, send_sem=ssem, recv_sem=rsem, device_id=where, device_id_type=MESH
        )

    front, back = iz > 0, iz < nz - 1
    to_back = remote(vol.at[planes - 1], zhalo.at[0], zs.at[0], zr.at[0], (ix, iy, iz + 1))
    to_front = remote(vol.at[0], zhalo.at[1], zs.at[1], zr.at[1], (ix, iy, iz - 1))

    @pl.when(back)
    def _():
        to_back.start()

    @pl.when(front)
    def _():
        to_front.start()

    build_tables(center_ref, table_ref, tab)

    source = lax.broadcasted_iota(jnp.int32, (across, across), 0)
    target = lax.broadcasted_iota(jnp.int32, (across, across), 1)
    gap = source - target
    blur = jnp.where(gap == 0, 2.0, jnp.where(jnp.abs(gap) == 1, 1.0, 0.0))
    slope = jnp.where(gap == 1, 1.0, jnp.where(gap == -1, -1.0, 0.0))
    stencil = jnp.concatenate([blur, slope], axis=1).astype(BF16)

    def edge_columns(cells, plane):
        right = jnp.where((source == across - 1) & (target == 2 * plane + 1), 1.0, 0.0)
        left = jnp.where((source == 0) & (target == 2 * plane), 1.0, 0.0)
        return jnp.dot(cells, (right + left).astype(BF16), preferred_element_type=F32)

    def own_plane(z, acc):
        cells = vol[z]
        xsd[z + 1, pl.ds(8, height), :] = jnp.dot(cells, stencil, preferred_element_type=F32)
        return acc + edge_columns(cells, z + 1)

    columns = lax.fori_loop(0, planes, own_plane, jnp.zeros((height, across), F32))

    @pl.when(back)
    def _():
        to_back.wait_send()
        to_front.wait_recv()

    @pl.when(front)
    def _():
        to_front.wait_send()
        to_back.wait_recv()

    @pl.when(jnp.logical_not(front))
    def _():
        zhalo[0] = jnp.zeros_like(zhalo[0])

    @pl.when(jnp.logical_not(back))
    def _():
        zhalo[1] = jnp.zeros_like(zhalo[1])

    for slot, plane in ((0, 0), (1, planes + 1)):
        cells = zhalo[slot]
        xsd[plane, pl.ds(8, height), :] = jnp.dot(cells, stencil, preferred_element_type=F32)
        columns = columns + edge_columns(cells, plane)
    face[...] = columns.astype(BF16)

    def edge_rows(row):
        own = vol[:, row, :].astype(F32)
        pad = jnp.zeros((rows_out.shape[1] - planes - 2, across), F32)
        ends = [zhalo[slot, row : row + 1, :].astype(F32) for slot in (0, 1)]
        return jnp.concatenate([ends[0], own, ends[1], pad], axis=0).astype(BF16)

    rows_out[0] = edge_rows(0)
    rows_out[1] = edge_rows(height - 1)

    halo = []
    for s, slot in ((1, 0), (-1, 1)):
        sending = (ix + s >= 0) & (ix + s < nx)
        taking = (ix - s >= 0) & (ix - s < nx)
        halo.append((sending, taking, remote(face, faces.at[slot], fs.at[slot], fr.at[slot], (ix + s, iy, iz))))
    for s, side in ((1, 0), (-1, 1)):
        for t in (-1, 0, 1):
            slot = 1 - t
            sending = (iy + s >= 0) & (iy + s < ny) & (ix + t >= 0) & (ix + t < nx)
            taking = (iy - s >= 0) & (iy - s < ny) & (ix - t >= 0) & (ix - t < nx)
            halo.append(
                (sending, taking, remote(rows_out.at[1 - side], rows_in.at[side, slot], rs.at[side, slot], rr.at[side, slot], (ix + t, iy + s, iz)))
            )
    for sending, _, copy in halo:

        @pl.when(sending)
        def _(copy=copy):
            copy.start()

    tall = 16

    def look_block(n, carry):
        z = n // (height // tall)
        row = pl.multiple_of((n % (height // tall)) * tall, tall)
        cells = vol[z, pl.ds(row, tall), :].astype(F32)
        for half in range(tall // 8):
            four = lookup(cells[8 * half : 8 * half + 8], tab)
            for c in range(4):
                look[c, z, pl.ds(row + 8 * half, 8), :] = four[c]
        return carry

    lax.fori_loop(0, planes * (height // tall), look_block, 0)

    for sending, taking, copy in halo:

        @pl.when(taking)
        def _(copy=copy):
            copy.wait_recv()

        @pl.when(sending)
        def _(copy=copy):
            copy.wait_send()

    lane = lax.broadcasted_iota(jnp.int32, (height, across), 1)
    both = jnp.where(lane % 2 == 1, faces[0].astype(F32), faces[1].astype(F32))
    ends = jnp.where((lane == 0) | (lane == across - 1), 1.0, 0.0)
    sign = jnp.where(lane == 0, -1.0, jnp.where(lane == across - 1, 1.0, 0.0))

    def add_columns(z, carry):
        placed = pltpu.roll(both, across - 2 * z - 1, 1)
        xsd[z, pl.ds(8, height), :] += jnp.concatenate([placed * ends, placed * sign], axis=1)
        return carry

    lax.fori_loop(0, planes + 2, add_columns, 0)
    count_rows = rows_out.shape[1]
    for side in (0, 1):
        strip = jnp.dot(rows_in[side, 1], stencil, preferred_element_type=F32)
        left = pltpu.roll(rows_in[side, 0].astype(F32), 1, 1)
        right = pltpu.roll(rows_in[side, 2].astype(F32), across - 1, 1)
        short = lax.broadcasted_iota(jnp.int32, (count_rows, across), 1)
        left = jnp.where(short == 0, left, 0.0)
        right = jnp.where(short == across - 1, right, 0.0)
        strip = strip + jnp.concatenate([left + right, right - left], axis=1)
        row = 7 if side == 0 else 8 + height
        for z in range(planes + 2):
            xsd[z, row : row + 1, :] = strip[z : z + 1]

    shade_scale = (1.0 - ambient) / (32.0 * 3.0**0.5)

    sub = lax.broadcasted_iota(jnp.int32, (8, 2 * across), 0)

    def march(row):
        def gradients(z):
            above = xsd[z, pl.ds(row, 8), :]
            mid = xsd[z, pl.ds(row + 8, 8), :]
            below = xsd[z, pl.ds(row + 16, 8), :]
            up = pltpu.roll(jnp.where(sub == 7, above, mid), 1, 0)
            down = pltpu.roll(jnp.where(sub == 0, below, mid), 7, 0)
            smoothed = up + 2.0 * mid + down
            return smoothed[:, across:], down[:, :across] - up[:, :across], smoothed[:, :across]

        through = jnp.ones((8, across), F32)
        sums = [jnp.zeros((8, across), F32) for _ in range(3)]
        before, here = gradients(0), gradients(1)
        for z in range(planes):
            after = gradients(z + 2)
            grad_x = before[0] + 2.0 * here[0] + after[0]
            grad_y = before[1] + 2.0 * here[1] + after[1]
            grad_z = after[2] - before[2]
            before, here = here, after
            square = (grad_x * grad_x + grad_y * grad_y + grad_z * grad_z) * (1.0 / 1024.0) + grad_floor
            shade = ambient + shade_scale * jnp.abs(grad_x + grad_y + grad_z) * lax.rsqrt(square)
            clear = jnp.exp(look[3, z, pl.ds(row, 8), :] * (-depth_scale / depth))
            weight = through * (1.0 - clear) * shade
            for c in range(3):
                sums[c] = sums[c] + weight * look[c, z, pl.ds(row, 8), :]
            through = through * clear
        for c in range(3):
            part[c, pl.ds(row, 8), :] = sums[c]
        part[3, pl.ds(row, 8), :] = through

    half = height // 2
    band = height // 4
    keep = bit0 * half
    give = (1 - bit0) * half

    def march_half(start):
        def step(n, carry):
            march(pl.multiple_of(start + 8 * n, 8))
            return carry

        lax.fori_loop(0, half // 8, step, 0)

    march_half(give)
    first = remote(part.at[:, pl.ds(pl.multiple_of(give, half), half), :], recv1, es.at[0], er.at[0], (ix, iy, near))
    first.start()
    march_half(keep)
    first.wait_recv()

    def fold(mine, theirs, i_am_front):
        ahead = jnp.where(i_am_front, mine[3], theirs[3])
        mixed = []
        for c in range(3):
            a = jnp.where(i_am_front, mine[c], theirs[c])
            b = jnp.where(i_am_front, theirs[c], mine[c])
            mixed.append(a + ahead * b)
        mixed.append(mine[3] * theirs[3])
        return mixed

    pair = fold([part[c, pl.ds(pl.multiple_of(keep, half), half), :] for c in range(4)], [recv1[c] for c in range(4)], bit0 == 0)
    for c in range(4):
        bit_a[c] = pair[c]
    keep2 = pl.multiple_of(bit1 * band, band)
    give2 = pl.multiple_of((1 - bit1) * band, band)
    second = remote(bit_a.at[:, pl.ds(give2, band), :], recv2, es.at[1], er.at[1], (ix, iy, far))
    second.start()
    second.wait_recv()
    quad = fold([bit_a[c, pl.ds(keep2, band), :] for c in range(4)], [recv2[c] for c in range(4)], bit1 == 0)
    quad[3] = 1.0 - quad[3]

    def region(j, z):
        b = (z % 2) * 2 + z // 2
        return out.at[:, pl.ds(pl.multiple_of(b * band, band), band), pl.ds(pl.multiple_of(j * across, across), across)]

    mine_ref = region(ix, iz)
    for c in range(4):
        mine_ref[c] = quad[c]

    def up(j, t):
        return remote(region(j, iz), region(j, iz), us.at[t], ur.at[t], (ix + 1, iy, iz))

    def down(j, t):
        return remote(region(j, iz), region(j, iz), ds.at[t], dr.at[t], (ix - 1, iy, iz))

    def over(j, slot):
        return remote(region(j, iz), region(j, iz), ys.at[slot], yr.at[slot], (ix, iy, far))

    def side(j, slot):
        return remote(region(j, iz), region(j, iz), cs.at[slot], cr.at[slot], (ix, iy, near))

    def side_far(j, slot):
        return remote(region(j, far), region(j, far), qs.at[slot], qr.at[slot], (ix, iy, near))

    def take_over(j, slot):
        return remote(region(j, far), region(j, far), ys.at[slot], yr.at[slot], (ix, iy, far))

    far_near = near + 2 - 4 * bit1

    def spread(j, t, slot, upward, downward):
        if upward and t < nx - 1:

            @pl.when(ix + 1 < nx)
            def _():
                up(j, t).start()

        if downward and t < nx - 1:

            @pl.when(ix >= 1)
            def _():
                down(j, t).start()

        over(j, slot).start()
        side(j, slot).start()

    def relay(j, slot):
        take_over(j, slot).wait_recv()
        side_far(j, slot).start()

    spread(ix, 0, 0, True, True)
    for t in range(1, nx):

        @pl.when(ix >= t)
        def _(t=t):
            up(ix - t, t - 1).wait_recv()
            spread(ix - t, t, 2 * t - 1, True, False)

        @pl.when(ix + t < nx)
        def _(t=t):
            down(ix + t, t - 1).wait_recv()
            spread(ix + t, t, 2 * t, False, True)

        if t == 1:
            relay(ix, 0)
        else:

            @pl.when(ix >= t - 1)
            def _(t=t):
                relay(ix - t + 1, 2 * t - 3)

            @pl.when(ix + t - 1 < nx)
            def _(t=t):
                relay(ix + t - 1, 2 * t - 2)

    if nx == 1:
        relay(ix, 0)
    else:

        @pl.when(ix >= nx - 1)
        def _():
            relay(ix - nx + 1, 2 * nx - 3)

        @pl.when(ix + nx - 1 < nx)
        def _():
            relay(ix + nx - 1, 2 * nx - 2)

    def finish(j, slot):
        over(j, slot).wait_send()
        side(j, slot).wait_send()
        side_far(j, slot).wait_send()
        remote(region(j, near), region(j, near), cs.at[slot], cr.at[slot], (ix, iy, near)).wait_recv()
        remote(region(j, far_near), region(j, far_near), qs.at[slot], qr.at[slot], (ix, iy, near)).wait_recv()

    finish(ix, 0)
    for t in range(1, nx):

        @pl.when(ix >= t)
        def _(t=t):
            finish(ix - t, 2 * t - 1)

        @pl.when(ix + t < nx)
        def _(t=t):
            finish(ix + t, 2 * t)

    for t in range(nx - 1):

        @pl.when((ix >= t) & (ix + 1 < nx))
        def _(t=t):
            up(ix - t, t).wait_send()

        @pl.when((ix + t < nx) & (ix >= 1))
        def _(t=t):
            down(ix + t, t).wait_send()

    first.wait_send()
    second.wait_send()


def shards(volume, hat_center, tf_table):
    planes, height, across = volume.shape
    sizes = tuple(lax.axis_size(a) for a in ("gx", "gy", "gz"))
    nx = sizes[0]
    assert sizes[2] == 4 and across == LANES
    extended_rows = -(-(planes + 2) // 16) * 16
    dma = pltpu.SemaphoreType.DMA
    vmem = pl.BlockSpec(memory_space=pltpu.VMEM)
    return pl.pallas_call(
        functools.partial(body, sizes),
        out_shape=jax.ShapeDtypeStruct((4, height, across * nx), F32),
        in_specs=[vmem] * 3,
        out_specs=vmem,
        scratch_shapes=[
            pltpu.VMEM((32, GROUPS * LANES), F32),
            pltpu.VMEM((planes + 2, height + 16, 2 * across), F32),
            pltpu.VMEM((4, planes, height, across), F32),
            pltpu.VMEM((2, height, across), BF16),
            pltpu.VMEM((height, across), BF16),
            pltpu.VMEM((2, height, across), BF16),
            pltpu.VMEM((2, extended_rows, across), BF16),
            pltpu.VMEM((2, 3, extended_rows, across), BF16),
            pltpu.VMEM((4, height, across), F32),
            pltpu.VMEM((4, height // 2, across), F32),
            pltpu.VMEM((4, height // 4, across), F32),
            pltpu.VMEM((4, height // 2, across), F32),
            dma((2,)), dma((2,)),
            dma((2,)), dma((2,)),
            dma((2, 3)), dma((2, 3)),
            dma((2,)), dma((2,)),
            dma((nx,)), dma((nx,)),
            dma((nx,)), dma((nx,)),
            dma((2 * nx,)), dma((2 * nx,)),
            dma((2 * nx,)), dma((2 * nx,)),
            dma((2 * nx,)), dma((2 * nx,)),
        ],
        compiler_params=pltpu.CompilerParams(collective_id=0, has_side_effects=True, vmem_limit_bytes=48 << 20),
    )(volume, hat_center.reshape(1, -1), tf_table)


def solution(mesh):
    in_specs = (P("gz", "gy", "gx"), P(), P())
    out_specs = P(None, "gy", None)
    return jax.shard_map(shards, mesh=mesh, in_specs=in_specs, out_specs=out_specs, check_vma=False)
```

time: 188 us -> 53.8 us (0.29)
  matrix products: 72.4 us -> 0 us
  Pallas kernels: 0 us -> 50.2 us
  waiting for transfers between devices: 44.7 us -> 0 us
  other arithmetic: 20.4 us -> 0 us
  starting transfers between devices: 13.8 us -> 0 us
  between operations: 13.6 us -> 0.01 us
  blocking collectives: 10 us -> 0 us
  local copies, waits for them, and re-layouts: 11.3 us -> 3.37 us
    dot_general x16 -> x0, matrix products: 72.4 us -> none  [colour(): return jnp.dot(tf_table, hat_values, preferred_element_type=jnp.float32)]
    pallas_call x0 -> x1, Pallas kernels: none -> 50.2 us  [shards(): pl.pallas_call(functools.partial(body, sizes), out_shape=jax.ShapeDtypeSt...]
    all_gather x1 -> x0, waiting for transfers between devices: 38.5 us -> none  [display(): stacked = lax.all_gather(band_piece[None], ('gx', 'gz'), axis=0, tiled=True)]
    ppermute x6 -> x0, starting transfers between devices: 13.8 us -> none  [the longest x3 9.68 us: extended(): lax.ppermute(tail, axis, [(i, (i + 1) % count) for i in range(ends)])]
    mul x17 -> x0, other arithmetic: 12.4 us -> none  [the longest x16 12.2 us: colour(): bin_level = voxels.astype(jnp.float32) * (NBIN - 1)]
    all_to_all x1 -> x0, blocking collectives: 10 us -> none  [shards(): lax.all_to_all(shaped, 'gz', split_axis=2, concat_axis=0, tiled=True)]
    reshape x3 -> x0, local copies, waits for them, and re-layouts: 7.54 us -> none  [the longest x1 6.14 us: shards(): transfer = transfer.reshape(planes, 4, height, across)]
    ppermute x6 -> x0, waiting for transfers between devices: 6.19 us -> none  [the longest x3 6.18 us: extended(): lax.ppermute(head, axis, [((i + 1) % count, i) for i in range(ends)])]
  transfers between devices with their start and end apart: 7 -> 0, of which waited for: 3 -> 0; matrix products, arithmetic and copies ran while one was open for 50% -> 0% of each run, Pallas kernels for 0% -> 0%
where the time goes in v1:
time: 53.8 us; the launch traced here: 53.6 us
  Pallas kernels  50.2 us (93%)
  local copies, waits for them, and re-layouts  3.37 us (6%)
    pallas_call x1, Pallas kernels, shards(): pl.pallas_call(functools.partial(body, sizes), out_shape=jax.ShapeDtypeSt...  50.2 us
    unnamed x7, local copies, waits for them, and re-layouts  3.37 us

profile of v1, /device:TPU:0, one launch (start us, length us, event | category | flops | bytes accessed | tf_op | source)
XLA Modules:
  0.0 53.6 jit_solution(3352482596977290616)
XLA Ops:
  0.0 0.0 copy-start.2
  0.0 0.7 %copy-done.2 = s32[256]{0:T(256)S(1)} copy-done((s32[256]{0:T(256)S(1)}, s32[256]{0:T(256)}, u32[]{:S(2)}) %copy-start.2) | copy-done | bytes 1048
  0.7 0.0 copy-start
  0.7 1.0 %copy-done = bf16[16,128,128]{2,1,0:T(8,128)(2,1)S(1)} copy-done((bf16[16,128,128]{2,1,0:T(8,128)(2,1)S(1)}, bf16[16,128,128]{2,1,0:T(8,128)(2,1)}, u32[]{:S(2)}) %copy-start) | copy-done | bytes 524312
  1.7 0.0 copy-start.1
  1.7 0.7 %copy-done.1 = bf16[4,256]{1,0:T(4,128)(2,1)S(1)} copy-done((bf16[4,256]{1,0:T(4,128)(2,1)S(1)}, bf16[4,256]{1,0:T(4,128)(2,1)}, u32[]{:S(2)}) %copy-start.1) | copy-done | bytes 2072
  2.4 50.2 %shard_map.37 = f32[4,128,512]{2,1,0:T(8,128)S(1)} custom-call(bf16[16,128,128]{2,1,0:T(8,128)(2,1)S(1)} %copy-done, s32[1,256]{1,0:T(1,128)S(1)} %bitcast.1, bf16[4,256]{1,0:T(4,128)(2,1)S(1)} %copy-done.1), custom_call_target="tpu_custom_call" | custom-call | tf_op jit(solution)/shard_map/pallas_call | solution.py:453
  52.6 1.0 %copy.5 = f32[4,128,512]{2,1,0:T(8,128)} copy(f32[4,128,512]{2,1,0:T(8,128)S(1)} %shard_map.37) | data formatting | bytes 2097152
Async XLA Ops:
  0.0 0.7 %copy-start.2 = (s32[256]{0:T(256)S(1)}, s32[256]{0:T(256)}, u32[]{:S(2)}) copy-start(s32[256]{0:T(256)} %param.4) | copy-start | bytes 3076
  0.7 1.0 %copy-start = (bf16[16,128,128]{2,1,0:T(8,128)(2,1)S(1)}, bf16[16,128,128]{2,1,0:T(8,128)(2,1)}, u32[]{:S(2)}) copy-start(bf16[16,128,128]{2,1,0:T(8,128)(2,1)} %vol.1) | copy-start | bytes 1572868
  1.7 0.7 %copy-start.1 = (bf16[4,256]{1,0:T(4,128)(2,1)S(1)}, bf16[4,256]{1,0:T(4,128)(2,1)}, u32[]{:S(2)}) copy-start(bf16[4,256]{1,0:T(4,128)(2,1)} %table_ref.1) | copy-start | bytes 6148

commit v2 on v1

--- a/solution.py
+++ b/solution.py
@@ -15,8 +15,7 @@
 depth_scale = 1.5
 
 LANES = 128
-BINADES = 8
-GROUPS = BINADES + 5
+GROUPS = 7
 MESH = pl.DeviceIdType.MESH
 F32 = jnp.float32
 BF16 = jnp.bfloat16
@@ -29,51 +28,53 @@
         [jnp.broadcast_to(wide[c : c + 1], (8, NBIN)) for c in range(4)], axis=0
     ).astype(BF16)
     centers = jnp.broadcast_to(centers, (LANES, NBIN))
-    step = lax.broadcasted_iota(jnp.int32, (LANES, NBIN), 0).astype(F32) + float(LANES)
+    row = lax.broadcasted_iota(jnp.int32, (LANES, NBIN), 0).astype(F32)
+    away = centers - row
 
     def hats(level):
         return jnp.maximum(0.0, 1.0 - jnp.abs(level - centers) / HW)
 
-    for group in range(GROUPS):
-        if group < BINADES:
-            weights = hats(step * (2.0 ** -(group + 8)) * (NBIN - 1))
-        elif group == BINADES:
-            weights = jnp.maximum(0.0, 1.0 - centers / HW)
-        elif group == BINADES + 1:
-            weights = jnp.where(centers == 0.0, -1.0, jnp.where(centers <= 2.0, 1.0, 0.0))
-        elif group == BINADES + 2:
-            weights = jnp.where(centers == 3.0, 1.0, 0.0)
-        elif group == BINADES + 3:
-            weights = jnp.where(centers == 4.0, 1.0, 0.0)
-        else:
-            weights = hats(jnp.full((LANES, NBIN), float(NBIN - 1), F32))
+    groups = [
+        hats((row + LANES) * (1.0 / (2 * LANES)) * (NBIN - 1)),
+        jnp.where(away == -3.0, 0.0, jnp.maximum(0.0, 1.0 - jnp.abs(away) / HW)),
+        jnp.where((away == 1.0) | (away == 2.0), 1.0, jnp.where((away == 0.0) | (away == -1.0), -1.0, 0.0)),
+        jnp.where(away == 3.0, 1.0, jnp.where(away == -2.0, -1.0, 0.0)),
+        jnp.where(away == 4.0, 1.0, 0.0),
+        jnp.where(away == -3.0, 1.0, 0.0),
+        hats(jnp.full((LANES, NBIN), float(NBIN - 1), F32)),
+    ]
+    for group, weights in enumerate(groups):
         tab[:, group * LANES : (group + 1) * LANES] = lax.dot_general(
             copies, weights.astype(BF16), (((1,), (1,)), ((), ())), preferred_element_type=F32
         )
 
 
 def lookup(values, tab):
-    masks = [values >= 2.0 ** -(k + 1) for k in range(BINADES)]
-    scale = jnp.full(values.shape, 2.0 ** (BINADES + 7), F32)
-    for k in range(BINADES - 2, -1, -1):
-        scale = jnp.where(masks[k], 2.0 ** (k + 8), scale)
-    index = (values * scale).astype(jnp.int32) & (LANES - 1)
-    quarter = values * ((NBIN - 1) / 4.0)
+    level = values * float(NBIN - 1)
+    bin_index = level.astype(jnp.int32)
+    part_bin = level - bin_index.astype(F32)
+    quarter = part_bin * 0.25
     coarse = (quarter + 1.5 * 2.0**15) - 1.5 * 2.0**15
     fine = (quarter + 1.5 * 2.0**14) - 1.5 * 2.0**14
-    finest = quarter.astype(BF16).astype(F32)
-    top = values >= 1.0
+    rising = quarter.astype(BF16).astype(F32)
+    falling = ((1.0 - part_bin) * 0.25).astype(BF16).astype(F32)
+    low_index = bin_index & (LANES - 1)
+    high_index = (values * float(2 * LANES)).astype(jnp.int32) & (LANES - 1)
+    upper, top = values >= 0.5, values >= 1.0
+
+    def entry(c, group):
+        return tab[8 * c : 8 * c + 8, group * LANES : (group + 1) * LANES]
+
     out = []
     for c in range(4):
-
-        def entry(group):
-            return tab[8 * c : 8 * c + 8, group * LANES : (group + 1) * LANES]
-
-        total = entry(BINADES) + coarse * entry(BINADES + 1)
-        total = total + fine * entry(BINADES + 2) + finest * entry(BINADES + 3)
-        for k in range(BINADES - 1, -1, -1):
-            total = jnp.where(masks[k], jnp.take_along_axis(entry(k), index, axis=1), total)
-        out.append(jnp.where(top, entry(BINADES + 4), total))
+        flat, per_coarse, per_fine, per_rising, per_falling = (
+            jnp.take_along_axis(entry(c, 1 + k), low_index, axis=1) for k in range(5)
+        )
+        total = (flat + coarse * per_coarse) + (fine * per_fine + rising * per_rising + falling * per_falling)
+        out.append(total)
+    for c in range(4):
+        high = jnp.take_along_axis(entry(c, 0), high_index, axis=1)
+        out[c] = jnp.where(top, entry(c, 6), jnp.where(upper, high, out[c]))
     return out
 
 
@@ -204,7 +205,7 @@
         def _(copy=copy):
             copy.start()
 
-    tall = 16
+    tall = 64
 
     def look_block(n, carry):
         z = n // (height // tall)

time: 53.8 us -> 44.3 us (0.82)
  Pallas kernels: 50.2 us -> 40.7 us
    pallas_call x1, Pallas kernels: 50.2 us -> 40.7 us  [shards(): pl.pallas_call(functools.partial(body, sizes), out_shape=jax.ShapeDtypeSt...]
where the time goes in v2:
time: 44.3 us; the launch traced here: 44.1 us
  Pallas kernels  40.7 us (92%)
  local copies, waits for them, and re-layouts  3.37 us (8%)
    pallas_call x1, Pallas kernels, shards(): pl.pallas_call(functools.partial(body, sizes), out_shape=jax.ShapeDtypeSt...  40.7 us
    unnamed x7, local copies, waits for them, and re-layouts  3.37 us

profile of v2, /device:TPU:0, one launch (start us, length us, event | category | flops | bytes accessed | tf_op | source)
XLA Modules:
  0.0 44.1 jit_solution(10364880049423432749)
XLA Ops:
  0.0 0.0 copy-start.2
  0.0 0.7 %copy-done.2 = s32[256]{0:T(256)S(1)} copy-done((s32[256]{0:T(256)S(1)}, s32[256]{0:T(256)}, u32[]{:S(2)}) %copy-start.2) | copy-done | bytes 1048
  0.7 0.0 copy-start
  0.7 1.0 %copy-done = bf16[16,128,128]{2,1,0:T(8,128)(2,1)S(1)} copy-done((bf16[16,128,128]{2,1,0:T(8,128)(2,1)S(1)}, bf16[16,128,128]{2,1,0:T(8,128)(2,1)}, u32[]{:S(2)}) %copy-start) | copy-done | bytes 524312
  1.7 0.0 copy-start.1
  1.7 0.7 %copy-done.1 = bf16[4,256]{1,0:T(4,128)(2,1)S(1)} copy-done((bf16[4,256]{1,0:T(4,128)(2,1)S(1)}, bf16[4,256]{1,0:T(4,128)(2,1)}, u32[]{:S(2)}) %copy-start.1) | copy-done | bytes 2072
  2.4 40.7 %shard_map.37 = f32[4,128,512]{2,1,0:T(8,128)S(1)} custom-call(bf16[16,128,128]{2,1,0:T(8,128)(2,1)S(1)} %copy-done, s32[1,256]{1,0:T(1,128)S(1)} %bitcast.1, bf16[4,256]{1,0:T(4,128)(2,1)S(1)} %copy-done.1), custom_call_target="tpu_custom_call" | custom-call | tf_op jit(solution)/shard_map/pallas_call | solution.py:454
  43.1 1.0 %copy.5 = f32[4,128,512]{2,1,0:T(8,128)} copy(f32[4,128,512]{2,1,0:T(8,128)S(1)} %shard_map.37) | data formatting | bytes 2097152
Async XLA Ops:
  0.0 0.7 %copy-start.2 = (s32[256]{0:T(256)S(1)}, s32[256]{0:T(256)}, u32[]{:S(2)}) copy-start(s32[256]{0:T(256)} %param.4) | copy-start | bytes 3076
  0.7 1.0 %copy-start = (bf16[16,128,128]{2,1,0:T(8,128)(2,1)S(1)}, bf16[16,128,128]{2,1,0:T(8,128)(2,1)}, u32[]{:S(2)}) copy-start(bf16[16,128,128]{2,1,0:T(8,128)(2,1)} %vol.1) | copy-start | bytes 1572868
  1.7 0.7 %copy-start.1 = (bf16[4,256]{1,0:T(4,128)(2,1)S(1)}, bf16[4,256]{1,0:T(4,128)(2,1)}, u32[]{:S(2)}) copy-start(bf16[4,256]{1,0:T(4,128)(2,1)} %table_ref.1) | copy-start | bytes 6148

commit v3 on v2

--- a/solution.py
+++ b/solution.py
@@ -78,7 +78,7 @@
     return out
 
 
-def body(sizes, vol, center_ref, table_ref, out, tab, xsd, look, zhalo, face, faces, rows_out, rows_in, part, recv1, recv2, bit_a,
+def body(sizes, vol, center_ref, table_ref, out, tab, xsd, look_a, look_b, look_c, zhalo, face, faces, rows_out, rows_in, part, recv1, recv2, pair,
          zs, zr, fs, fr, rs, rr, es, er, us, ur, ds, dr, ys, yr, cs, cr, qs, qr):
     nx, ny, nz = sizes
     planes, height, across = vol.shape
@@ -205,19 +205,22 @@
         def _(copy=copy):
             copy.start()
 
-    tall = 64
-
-    def look_block(n, carry):
-        z = n // (height // tall)
-        row = pl.multiple_of((n % (height // tall)) * tall, tall)
-        cells = vol[z, pl.ds(row, tall), :].astype(F32)
-        for half in range(tall // 8):
-            four = lookup(cells[8 * half : 8 * half + 8], tab)
+    half, band = height // 2, height // 4
+    keep, give = bit0 * half, (1 - bit0) * half
+    keep2, give2 = bit1 * band, (1 - bit1) * band
+
+    def look_rows(table, z, start, count):
+        cells = vol[z, pl.ds(pl.multiple_of(start, 16), count), :].astype(F32)
+        for k in range(count // 8):
+            four = lookup(cells[8 * k : 8 * k + 8], tab)
             for c in range(4):
-                look[c, z, pl.ds(row + 8 * half, 8), :] = four[c]
+                table[c, z, 8 * k : 8 * k + 8, :] = four[c]
+
+    def look_give(z, carry):
+        look_rows(look_a, z, give, half)
         return carry
 
-    lax.fori_loop(0, planes * (height // tall), look_block, 0)
+    lax.fori_loop(0, planes, look_give, 0)
 
     for sending, taking, copy in halo:
 
@@ -257,7 +260,7 @@
 
     sub = lax.broadcasted_iota(jnp.int32, (8, 2 * across), 0)
 
-    def march(row):
+    def march(row, table, own):
         def gradients(z):
             above = xsd[z, pl.ds(row, 8), :]
             mid = xsd[z, pl.ds(row + 8, 8), :]
@@ -278,31 +281,34 @@
             before, here = here, after
             square = (grad_x * grad_x + grad_y * grad_y + grad_z * grad_z) * (1.0 / 1024.0) + grad_floor
             shade = ambient + shade_scale * jnp.abs(grad_x + grad_y + grad_z) * lax.rsqrt(square)
-            clear = jnp.exp(look[3, z, pl.ds(row, 8), :] * (-depth_scale / depth))
+            clear = jnp.exp(table[3, z, pl.ds(own, 8), :] * (-depth_scale / depth))
             weight = through * (1.0 - clear) * shade
             for c in range(3):
-                sums[c] = sums[c] + weight * look[c, z, pl.ds(row, 8), :]
+                sums[c] = sums[c] + weight * table[c, z, pl.ds(own, 8), :]
             through = through * clear
         for c in range(3):
             part[c, pl.ds(row, 8), :] = sums[c]
         part[3, pl.ds(row, 8), :] = through
 
-    half = height // 2
-    band = height // 4
-    keep = bit0 * half
-    give = (1 - bit0) * half
-
-    def march_half(start):
+    def march_rows(start, table, count, along=None):
         def step(n, carry):
-            march(pl.multiple_of(start + 8 * n, 8))
+            march(pl.multiple_of(start + 8 * n, 8), table, pl.multiple_of(8 * n, 8))
+            if along is not None:
+                along(n)
             return carry
 
-        lax.fori_loop(0, half // 8, step, 0)
-
-    march_half(give)
+        lax.fori_loop(0, count // 8, step, 0)
+
+    share = planes // (half // 8)
+
+    def look_give2(n):
+        for k in range(share):
+            look_rows(look_b, share * n + k, keep + give2, band)
+
+    march_rows(give, look_a, half, look_give2)
     first = remote(part.at[:, pl.ds(pl.multiple_of(give, half), half), :], recv1, es.at[0], er.at[0], (ix, iy, near))
     first.start()
-    march_half(keep)
+    march_rows(keep + give2, look_b, band)
     first.wait_recv()
 
     def fold(mine, theirs, i_am_front):
@@ -315,15 +321,26 @@
         mixed.append(mine[3] * theirs[3])
         return mixed
 
-    pair = fold([part[c, pl.ds(pl.multiple_of(keep, half), half), :] for c in range(4)], [recv1[c] for c in range(4)], bit0 == 0)
-    for c in range(4):
-        bit_a[c] = pair[c]
-    keep2 = pl.multiple_of(bit1 * band, band)
-    give2 = pl.multiple_of((1 - bit1) * band, band)
-    second = remote(bit_a.at[:, pl.ds(give2, band), :], recv2, es.at[1], er.at[1], (ix, iy, far))
+    def pair_of(start):
+        own = pl.ds(pl.multiple_of(keep + start, band), band)
+        other = pl.ds(pl.multiple_of(start, band), band)
+        return fold([part[c, own, :] for c in range(4)], [recv1[c, other, :] for c in range(4)], bit0 == 0)
+
+    for c, value in enumerate(pair_of(give2)):
+        pair[c] = value
+    second = remote(pair, recv2, es.at[1], er.at[1], (ix, iy, far))
     second.start()
+
+    def look_keep2(n, carry):
+        for k in range(2):
+            look_rows(look_c, 2 * n + k, keep + keep2, band)
+        return carry
+
+    lax.fori_loop(0, planes // 2, look_keep2, 0)
+    march_rows(keep + keep2, look_c, band)
+    mine = pair_of(keep2)
     second.wait_recv()
-    quad = fold([bit_a[c, pl.ds(keep2, band), :] for c in range(4)], [recv2[c] for c in range(4)], bit1 == 0)
+    quad = fold(mine, [recv2[c] for c in range(4)], bit1 == 0)
     quad[3] = 1.0 - quad[3]
 
     def region(j, z):
@@ -459,7 +476,9 @@
         scratch_shapes=[
             pltpu.VMEM((32, GROUPS * LANES), F32),
             pltpu.VMEM((planes + 2, height + 16, 2 * across), F32),
-            pltpu.VMEM((4, planes, height, across), F32),
+            pltpu.VMEM((4, planes, height // 2, across), F32),
+            pltpu.VMEM((4, planes, height // 4, across), F32),
+            pltpu.VMEM((4, planes, height // 4, across), F32),
             pltpu.VMEM((2, height, across), BF16),
             pltpu.VMEM((height, across), BF16),
             pltpu.VMEM((2, height, across), BF16),
@@ -468,7 +487,7 @@
             pltpu.VMEM((4, height, across), F32),
             pltpu.VMEM((4, height // 2, across), F32),
             pltpu.VMEM((4, height // 4, across), F32),
-            pltpu.VMEM((4, height // 2, across), F32),
+            pltpu.VMEM((4, height // 4, across), F32),
             dma((2,)), dma((2,)),
             dma((2,)), dma((2,)),
             dma((2, 3)), dma((2, 3)),

time: 44.3 us -> 41.6 us (0.939)
  Pallas kernels: 40.7 us -> 38 us
    pallas_call x1, Pallas kernels: 40.7 us -> 38 us  [shards(): pl.pallas_call(functools.partial(body, sizes), out_shape=jax.ShapeDtypeSt...]
where the time goes in v3:
time: 41.6 us; the launch traced here: 41.4 us
  Pallas kernels  38 us (91%)
  local copies, waits for them, and re-layouts  3.37 us (8%)
    pallas_call x1, Pallas kernels, shards(): pl.pallas_call(functools.partial(body, sizes), out_shape=jax.ShapeDtypeSt...  38 us
    unnamed x7, local copies, waits for them, and re-layouts  3.37 us

profile of v3, /device:TPU:0, one launch (start us, length us, event | category | flops | bytes accessed | tf_op | source)
XLA Modules:
  0.0 41.4 jit_solution(4058742098839935230)
XLA Ops:
  0.0 0.0 copy-start.2
  0.0 0.7 %copy-done.2 = s32[256]{0:T(256)S(1)} copy-done((s32[256]{0:T(256)S(1)}, s32[256]{0:T(256)}, u32[]{:S(2)}) %copy-start.2) | copy-done | bytes 1048
  0.7 0.0 copy-start
  0.7 1.0 %copy-done = bf16[16,128,128]{2,1,0:T(8,128)(2,1)S(1)} copy-done((bf16[16,128,128]{2,1,0:T(8,128)(2,1)S(1)}, bf16[16,128,128]{2,1,0:T(8,128)(2,1)}, u32[]{:S(2)}) %copy-start) | copy-done | bytes 524312
  1.7 0.0 copy-start.1
  1.7 0.7 %copy-done.1 = bf16[4,256]{1,0:T(4,128)(2,1)S(1)} copy-done((bf16[4,256]{1,0:T(4,128)(2,1)S(1)}, bf16[4,256]{1,0:T(4,128)(2,1)}, u32[]{:S(2)}) %copy-start.1) | copy-done | bytes 2072
  2.4 38.0 %shard_map.37 = f32[4,128,512]{2,1,0:T(8,128)S(1)} custom-call(bf16[16,128,128]{2,1,0:T(8,128)(2,1)S(1)} %copy-done, s32[1,256]{1,0:T(1,128)S(1)} %bitcast.1, bf16[4,256]{1,0:T(4,128)(2,1)S(1)} %copy-done.1), custom_call_target="tpu_custom_call" | custom-call | tf_op jit(solution)/shard_map/pallas_call | solution.py:471
  40.4 1.0 %copy.5 = f32[4,128,512]{2,1,0:T(8,128)} copy(f32[4,128,512]{2,1,0:T(8,128)S(1)} %shard_map.37) | data formatting | bytes 2097152
Async XLA Ops:
  0.0 0.7 %copy-start.2 = (s32[256]{0:T(256)S(1)}, s32[256]{0:T(256)}, u32[]{:S(2)}) copy-start(s32[256]{0:T(256)} %param.4) | copy-start | bytes 3076
  0.7 1.0 %copy-start = (bf16[16,128,128]{2,1,0:T(8,128)(2,1)S(1)}, bf16[16,128,128]{2,1,0:T(8,128)(2,1)}, u32[]{:S(2)}) copy-start(bf16[16,128,128]{2,1,0:T(8,128)(2,1)} %vol.1) | copy-start | bytes 1572868
  1.7 0.7 %copy-start.1 = (bf16[4,256]{1,0:T(4,128)(2,1)S(1)}, bf16[4,256]{1,0:T(4,128)(2,1)}, u32[]{:S(2)}) copy-start(bf16[4,256]{1,0:T(4,128)(2,1)} %table_ref.1) | copy-start | bytes 6148

commit v4 on v3

--- a/solution.py
+++ b/solution.py
@@ -343,66 +343,68 @@
     quad = fold(mine, [recv2[c] for c in range(4)], bit1 == 0)
     quad[3] = 1.0 - quad[3]
 
-    def region(j, z):
+    def region(j, z, h):
         b = (z % 2) * 2 + z // 2
-        return out.at[:, pl.ds(pl.multiple_of(b * band, band), band), pl.ds(pl.multiple_of(j * across, across), across)]
-
-    mine_ref = region(ix, iz)
+        return out.at[2 * h : 2 * h + 2, pl.ds(pl.multiple_of(b * band, band), band), pl.ds(pl.multiple_of(j * across, across), across)]
+
     for c in range(4):
-        mine_ref[c] = quad[c]
-
-    def up(j, t):
-        return remote(region(j, iz), region(j, iz), us.at[t], ur.at[t], (ix + 1, iy, iz))
-
-    def down(j, t):
-        return remote(region(j, iz), region(j, iz), ds.at[t], dr.at[t], (ix - 1, iy, iz))
-
-    def over(j, slot):
-        return remote(region(j, iz), region(j, iz), ys.at[slot], yr.at[slot], (ix, iy, far))
-
-    def side(j, slot):
-        return remote(region(j, iz), region(j, iz), cs.at[slot], cr.at[slot], (ix, iy, near))
-
-    def side_far(j, slot):
-        return remote(region(j, far), region(j, far), qs.at[slot], qr.at[slot], (ix, iy, near))
-
-    def take_over(j, slot):
-        return remote(region(j, far), region(j, far), ys.at[slot], yr.at[slot], (ix, iy, far))
+        region(ix, iz, c // 2)[c % 2] = quad[c]
+
+    def up(j, t, h):
+        return remote(region(j, iz, h), region(j, iz, h), us.at[t, h], ur.at[t, h], (ix + 1, iy, iz))
+
+    def down(j, t, h):
+        return remote(region(j, iz, h), region(j, iz, h), ds.at[t, h], dr.at[t, h], (ix - 1, iy, iz))
+
+    def over(j, slot, h):
+        return remote(region(j, iz, h), region(j, iz, h), ys.at[slot, h], yr.at[slot, h], (ix, iy, far))
+
+    def side(j, slot, h):
+        return remote(region(j, iz, h), region(j, iz, h), cs.at[slot, h], cr.at[slot, h], (ix, iy, near))
+
+    def side_far(j, slot, h):
+        return remote(region(j, far, h), region(j, far, h), qs.at[slot, h], qr.at[slot, h], (ix, iy, near))
+
+    def take_over(j, slot, h):
+        return remote(region(j, far, h), region(j, far, h), ys.at[slot, h], yr.at[slot, h], (ix, iy, far))
 
     far_near = near + 2 - 4 * bit1
 
-    def spread(j, t, slot, upward, downward):
+    def spread(j, t, slot, h, upward, downward):
         if upward and t < nx - 1:
 
             @pl.when(ix + 1 < nx)
             def _():
-                up(j, t).start()
+                up(j, t, h).start()
 
         if downward and t < nx - 1:
 
             @pl.when(ix >= 1)
             def _():
-                down(j, t).start()
-
-        over(j, slot).start()
-        side(j, slot).start()
+                down(j, t, h).start()
+
+        over(j, slot, h).start()
+        side(j, slot, h).start()
 
     def relay(j, slot):
-        take_over(j, slot).wait_recv()
-        side_far(j, slot).start()
-
-    spread(ix, 0, 0, True, True)
+        for h in range(2):
+            take_over(j, slot, h).wait_recv()
+            side_far(j, slot, h).start()
+
+    for h in range(2):
+        spread(ix, 0, 0, h, True, True)
     for t in range(1, nx):
-
-        @pl.when(ix >= t)
-        def _(t=t):
-            up(ix - t, t - 1).wait_recv()
-            spread(ix - t, t, 2 * t - 1, True, False)
-
-        @pl.when(ix + t < nx)
-        def _(t=t):
-            down(ix + t, t - 1).wait_recv()
-            spread(ix + t, t, 2 * t, False, True)
+        for h in range(2):
+
+            @pl.when(ix >= t)
+            def _(t=t, h=h):
+                up(ix - t, t - 1, h).wait_recv()
+                spread(ix - t, t, 2 * t - 1, h, True, False)
+
+            @pl.when(ix + t < nx)
+            def _(t=t, h=h):
+                down(ix + t, t - 1, h).wait_recv()
+                spread(ix + t, t, 2 * t, h, False, True)
 
         if t == 1:
             relay(ix, 0)
@@ -429,11 +431,13 @@
             relay(ix + nx - 1, 2 * nx - 2)
 
     def finish(j, slot):
-        over(j, slot).wait_send()
-        side(j, slot).wait_send()
-        side_far(j, slot).wait_send()
-        remote(region(j, near), region(j, near), cs.at[slot], cr.at[slot], (ix, iy, near)).wait_recv()
-        remote(region(j, far_near), region(j, far_near), qs.at[slot], qr.at[slot], (ix, iy, near)).wait_recv()
+        for h in range(2):
+            over(j, slot, h).wait_send()
+            side(j, slot, h).wait_send()
+            side_far(j, slot, h).wait_send()
+            ours, others = region(j, near, h), region(j, far_near, h)
+            remote(ours, ours, cs.at[slot, h], cr.at[slot, h], (ix, iy, near)).wait_recv()
+            remote(others, others, qs.at[slot, h], qr.at[slot, h], (ix, iy, near)).wait_recv()
 
     finish(ix, 0)
     for t in range(1, nx):
@@ -450,11 +454,13 @@
 
         @pl.when((ix >= t) & (ix + 1 < nx))
         def _(t=t):
-            up(ix - t, t).wait_send()
+            for h in range(2):
+                up(ix - t, t, h).wait_send()
 
         @pl.when((ix + t < nx) & (ix >= 1))
         def _(t=t):
-            down(ix + t, t).wait_send()
+            for h in range(2):
+                down(ix + t, t, h).wait_send()
 
     first.wait_send()
     second.wait_send()
@@ -492,11 +498,11 @@
             dma((2,)), dma((2,)),
             dma((2, 3)), dma((2, 3)),
             dma((2,)), dma((2,)),
-            dma((nx,)), dma((nx,)),
-            dma((nx,)), dma((nx,)),
-            dma((2 * nx,)), dma((2 * nx,)),
-            dma((2 * nx,)), dma((2 * nx,)),
-            dma((2 * nx,)), dma((2 * nx,)),
+            dma((nx, 2)), dma((nx, 2)),
+            dma((nx, 2)), dma((nx, 2)),
+            dma((2 * nx, 2)), dma((2 * nx, 2)),
+            dma((2 * nx, 2)), dma((2 * nx, 2)),
+            dma((2 * nx, 2)), dma((2 * nx, 2)),
         ],
         compiler_params=pltpu.CompilerParams(collective_id=0, has_side_effects=True, vmem_limit_bytes=48 << 20),
     )(volume, hat_center.reshape(1, -1), tf_table)

time: 41.6 us -> 41.1 us (0.988)
  Pallas kernels: 38 us -> 37.5 us
    pallas_call x1, Pallas kernels: 38 us -> 37.5 us  [shards(): pl.pallas_call(functools.partial(body, sizes), out_shape=jax.ShapeDtypeSt...]
where the time goes in v4:
time: 41.1 us; the launch traced here: 40.9 us
  Pallas kernels  37.5 us (91%)
  local copies, waits for them, and re-layouts  3.37 us (8%)
    pallas_call x1, Pallas kernels, shards(): pl.pallas_call(functools.partial(body, sizes), out_shape=jax.ShapeDtypeSt...  37.5 us
    unnamed x7, local copies, waits for them, and re-layouts  3.37 us

profile of v4, /device:TPU:0, one launch (start us, length us, event | category | flops | bytes accessed | tf_op | source)
XLA Modules:
  0.0 40.9 jit_solution(9210418359668454827)
XLA Ops:
  0.0 0.0 copy-start.2
  0.0 0.7 %copy-done.2 = s32[256]{0:T(256)S(1)} copy-done((s32[256]{0:T(256)S(1)}, s32[256]{0:T(256)}, u32[]{:S(2)}) %copy-start.2) | copy-done | bytes 1048
  0.7 0.0 copy-start
  0.7 1.0 %copy-done = bf16[16,128,128]{2,1,0:T(8,128)(2,1)S(1)} copy-done((bf16[16,128,128]{2,1,0:T(8,128)(2,1)S(1)}, bf16[16,128,128]{2,1,0:T(8,128)(2,1)}, u32[]{:S(2)}) %copy-start) | copy-done | bytes 524312
  1.7 0.0 copy-start.1
  1.7 0.7 %copy-done.1 = bf16[4,256]{1,0:T(4,128)(2,1)S(1)} copy-done((bf16[4,256]{1,0:T(4,128)(2,1)S(1)}, bf16[4,256]{1,0:T(4,128)(2,1)}, u32[]{:S(2)}) %copy-start.1) | copy-done | bytes 2072
  2.4 37.5 %shard_map.37 = f32[4,128,512]{2,1,0:T(8,128)S(1)} custom-call(bf16[16,128,128]{2,1,0:T(8,128)(2,1)S(1)} %copy-done, s32[1,256]{1,0:T(1,128)S(1)} %bitcast.1, bf16[4,256]{1,0:T(4,128)(2,1)S(1)} %copy-done.1), custom_call_target="tpu_custom_call" | custom-call | tf_op jit(solution)/shard_map/pallas_call | solution.py:477
  39.9 1.0 %copy.5 = f32[4,128,512]{2,1,0:T(8,128)} copy(f32[4,128,512]{2,1,0:T(8,128)S(1)} %shard_map.37) | data formatting | bytes 2097152
Async XLA Ops:
  0.0 0.7 %copy-start.2 = (s32[256]{0:T(256)S(1)}, s32[256]{0:T(256)}, u32[]{:S(2)}) copy-start(s32[256]{0:T(256)} %param.4) | copy-start | bytes 3076
  0.7 1.0 %copy-start = (bf16[16,128,128]{2,1,0:T(8,128)(2,1)S(1)}, bf16[16,128,128]{2,1,0:T(8,128)(2,1)}, u32[]{:S(2)}) copy-start(bf16[16,128,128]{2,1,0:T(8,128)(2,1)} %vol.1) | copy-start | bytes 1572868
  1.7 0.7 %copy-start.1 = (bf16[4,256]{1,0:T(4,128)(2,1)S(1)}, bf16[4,256]{1,0:T(4,128)(2,1)}, u32[]{:S(2)}) copy-start(bf16[4,256]{1,0:T(4,128)(2,1)} %table_ref.1) | copy-start | bytes 6148

commit v5 on v4

--- a/solution.py
+++ b/solution.py
@@ -308,7 +308,13 @@
     march_rows(give, look_a, half, look_give2)
     first = remote(part.at[:, pl.ds(pl.multiple_of(give, half), half), :], recv1, es.at[0], er.at[0], (ix, iy, near))
     first.start()
-    march_rows(keep + give2, look_b, band)
+
+    def look_keep2(n, carry):
+        for k in range(2):
+            look_rows(look_c, 2 * n + k, keep + keep2, band)
+        return carry
+
+    march_rows(keep + give2, look_b, band, lambda n: look_keep2(n, None))
     first.wait_recv()
 
     def fold(mine, theirs, i_am_front):
@@ -331,12 +337,7 @@
     second = remote(pair, recv2, es.at[1], er.at[1], (ix, iy, far))
     second.start()
 
-    def look_keep2(n, carry):
-        for k in range(2):
-            look_rows(look_c, 2 * n + k, keep + keep2, band)
-        return carry
-
-    lax.fori_loop(0, planes // 2, look_keep2, 0)
+    lax.fori_loop(band // 8, planes // 2, look_keep2, 0)
     march_rows(keep + keep2, look_c, band)
     mine = pair_of(keep2)
     second.wait_recv()

time: 41.1 us -> 41.3 us (level)
  no operation moved by 1% of the time
where the time goes in v5:
time: 41.3 us; the launch traced here: 41.1 us
  Pallas kernels  37.7 us (91%)
  local copies, waits for them, and re-layouts  3.37 us (8%)
    pallas_call x1, Pallas kernels, shards(): pl.pallas_call(functools.partial(body, sizes), out_shape=jax.ShapeDtypeSt...  37.7 us
    unnamed x7, local copies, waits for them, and re-layouts  3.37 us

profile of v5, /device:TPU:0, one launch (start us, length us, event | category | flops | bytes accessed | tf_op | source)
XLA Modules:
  0.0 41.1 jit_solution(12807825622086359272)
XLA Ops:
  0.0 0.0 copy-start.2
  0.0 0.7 %copy-done.2 = s32[256]{0:T(256)S(1)} copy-done((s32[256]{0:T(256)S(1)}, s32[256]{0:T(256)}, u32[]{:S(2)}) %copy-start.2) | copy-done | bytes 1048
  0.7 0.0 copy-start
  0.7 1.0 %copy-done = bf16[16,128,128]{2,1,0:T(8,128)(2,1)S(1)} copy-done((bf16[16,128,128]{2,1,0:T(8,128)(2,1)S(1)}, bf16[16,128,128]{2,1,0:T(8,128)(2,1)}, u32[]{:S(2)}) %copy-start) | copy-done | bytes 524312
  1.7 0.0 copy-start.1
  1.7 0.7 %copy-done.1 = bf16[4,256]{1,0:T(4,128)(2,1)S(1)} copy-done((bf16[4,256]{1,0:T(4,128)(2,1)S(1)}, bf16[4,256]{1,0:T(4,128)(2,1)}, u32[]{:S(2)}) %copy-start.1) | copy-done | bytes 2072
  2.4 37.7 %shard_map.37 = f32[4,128,512]{2,1,0:T(8,128)S(1)} custom-call(bf16[16,128,128]{2,1,0:T(8,128)(2,1)S(1)} %copy-done, s32[1,256]{1,0:T(1,128)S(1)} %bitcast.1, bf16[4,256]{1,0:T(4,128)(2,1)S(1)} %copy-done.1), custom_call_target="tpu_custom_call" | custom-call | tf_op jit(solution)/shard_map/pallas_call | solution.py:478
  40.2 1.0 %copy.5 = f32[4,128,512]{2,1,0:T(8,128)} copy(f32[4,128,512]{2,1,0:T(8,128)S(1)} %shard_map.37) | data formatting | bytes 2097152
Async XLA Ops:
  0.0 0.7 %copy-start.2 = (s32[256]{0:T(256)S(1)}, s32[256]{0:T(256)}, u32[]{:S(2)}) copy-start(s32[256]{0:T(256)} %param.4) | copy-start | bytes 3076
  0.7 1.0 %copy-start = (bf16[16,128,128]{2,1,0:T(8,128)(2,1)S(1)}, bf16[16,128,128]{2,1,0:T(8,128)(2,1)}, u32[]{:S(2)}) copy-start(bf16[16,128,128]{2,1,0:T(8,128)(2,1)} %vol.1) | copy-start | bytes 1572868
  1.7 0.7 %copy-start.1 = (bf16[4,256]{1,0:T(4,128)(2,1)S(1)}, bf16[4,256]{1,0:T(4,128)(2,1)}, u32[]{:S(2)}) copy-start(bf16[4,256]{1,0:T(4,128)(2,1)} %table_ref.1) | copy-start | bytes 6148
